TPU v7x, 32 devices: a whole 2x2x4 slice. The times are simulated.
32 devices in a mesh: dp: 8 (over z, y), mp: 4 (over x, core).
Axes of the slice: x: 2, y: 2, z: 4, core: 2. Of those that a mesh axis runs over, the one named last changes fastest.
Arguments:
- query: bfloat16 [4096, 4096], P('dp', 'mp'), may hold values from -6 to 6
- passage: bfloat16 [4096, 4096], P('dp', 'mp'), may hold values from -6 to 6
- query_scale: bfloat16 [4096], P('dp'), may hold values from 0.4 to 2.5
- passage_scale: bfloat16 [4096], P('dp'), may hold values from 0.4 to 2.5
- partners: int32 [8, 3], P('dp'), may hold values from 0 to 3, as said below
- counts: int32 [8], replicated, may hold values from 256 to 512, as said below
Outputs:
- loss: float32 [], replicated
- grad_query: bfloat16 [4096, 4096], P('dp', 'mp')
- grad_passage: bfloat16 [4096, 4096], P('dp', 'mp')
Inputs may be any that keep to these rules, and one draw needn't show every extreme that they name: `partners`: each nonzero entry of a row is a distinct distance; block 0 and the last 3 blocks use all 3 slots. `counts`: some block has all 512 rows valid.
All inputs are finite; a program needn't handle non-finite values.
Results may differ from a plain program's by a relative error of at most 0.004.
Values may be sent and summed in bfloat16 or wider, within the bound.
A program may use at most 64 MiB of HBM per device.

v0:
```python
import math

import jax
import jax.numpy as jnp
from jax import lax
from jax.sharding import PartitionSpec as P

D = 4096
WIN = 3


def shifted(value, axis, steps):
    count = lax.axis_size(axis)
    pairs = [(source, (source + steps) % count) for source in range(count)]
    return lax.ppermute(value, axis, pairs)


def local(query, passage, query_scale, passage_scale, partners, counts):
    inv = 1.0 / math.sqrt(D)
    rows = query.shape[0]
    mine = lax.axis_index("dp")
    ndev = lax.axis_size("dp")
    block_ids = jnp.arange(counts.shape[0], dtype=jnp.int32)

    def count_of(block):
        return jnp.sum(jnp.where(block_ids == block, counts, 0))

    far_rows = []
    far_scales = []
    far_counts = []
    for offset in range(1, WIN + 1):
        moved_rows, moved_scales = shifted((passage, passage_scale), "dp", -offset)
        far_rows.append(moved_rows)
        far_scales.append(moved_scales)
        far_counts.append(count_of((mine + offset) % ndev))
    offsets = partners[0]
    pick = jnp.clip(offsets - 1, 0, WIN - 1)
    keys = jnp.concatenate([passage[None], jnp.take(jnp.stack(far_rows), pick, axis=0)], axis=0)
    key_scales = jnp.concatenate(
        [passage_scale[None], jnp.take(jnp.stack(far_scales), pick, axis=0)], axis=0
    ).astype(jnp.float32)
    own_count = count_of(mine)
    key_counts = jnp.concatenate([own_count[None], jnp.take(jnp.stack(far_counts), pick)])
    live = jnp.concatenate([jnp.array([True]), offsets > 0])
    raw = jnp.einsum("id,kjd->kij", query, keys, preferred_element_type=jnp.float32)
    column = jnp.arange(rows, dtype=jnp.int32)
    col_ok = live[:, None] & (column[None, :] < key_counts[:, None])
    summed = lax.psum_scatter(raw, "mp", scatter_dimension=1, tiled=True)
    share = summed.shape[1]
    start = lax.axis_index("mp") * share
    row_ids = start + jnp.arange(share, dtype=jnp.int32)
    row_scale = lax.dynamic_slice_in_dim(query_scale, start, share).astype(jnp.float32)
    scores = summed * (row_scale * inv)[None, :, None] * key_scales[:, None, :]
    masked = jnp.where(col_ok[:, None, :], scores, -jnp.inf)
    top = jnp.max(masked, axis=(0, 2))
    weights = jnp.exp(masked - top[None, :, None])
    total = jnp.sum(weights, axis=(0, 2))
    lse = top + jnp.log(total)
    valid = row_ids < own_count
    diagonal = column[None, :] == row_ids[:, None]
    positive = jnp.sum(jnp.where(diagonal, scores[0], 0.0), axis=1)
    loss_rows = jnp.where(valid, lse - positive, 0.0)
    grads = weights / total[None, :, None]
    grads = jnp.concatenate([(grads[0] - diagonal.astype(jnp.float32))[None], grads[1:]], axis=0)
    grads = jnp.where(valid[None, :, None], grads, 0.0)
    key_weight = (grads * key_scales[:, None, :]).astype(jnp.bfloat16)
    row_weight = (grads * row_scale[None, :, None]).astype(jnp.bfloat16)
    loss_sum = jnp.sum(loss_rows)
    valid_sum = jnp.sum(valid.astype(jnp.float32))
    key_weight, row_weight = (
        lax.all_gather(key_weight, "mp", axis=1, tiled=True),
        lax.all_gather(row_weight, "mp", axis=1, tiled=True),
    )
    loss_all, valid_all = lax.psum((loss_sum, valid_sum), ("dp", "mp"))
    grad_query = jnp.einsum(
        "kij,kjd->id", key_weight, keys, preferred_element_type=jnp.float32
    ).astype(jnp.bfloat16)
    collected = jnp.einsum("ij,id->jd", row_weight[0], query, preferred_element_type=jnp.float32)
    far_parts = jnp.einsum(
        "kij,id->kjd", row_weight[1:], query, preferred_element_type=jnp.float32
    ).astype(jnp.bfloat16)
    for offset in range(1, WIN + 1):
        chosen = offsets == offset
        outgoing = jnp.sum(
            jnp.where(chosen[:, None, None], far_parts, jnp.zeros_like(far_parts)), axis=0
        )
        arrived = shifted(outgoing, "dp", offset)
        collected = collected + arrived.astype(jnp.float32)
    loss = loss_all / valid_all
    return (loss, grad_query, collected.astype(jnp.bfloat16))


def solution(mesh):
    return jax.shard_map(
        local,
        mesh=mesh,
        in_specs=(P("dp", "mp"), P("dp", "mp"), P("dp"), P("dp"), P("dp", None), P()),
        out_specs=(P(), P("dp", "mp"), P("dp", "mp")),
        check_vma=False,
    )
```

profile of v0, /device:TPU:0, one launch (start us, length us, event | category | flops | bytes accessed | tf_op | source)
XLA Modules:
  0.0 335.3 jit_solution(15261544324831672226)
XLA Ops:
  7.2 5.1 %collective-permute-start.2 = (bf16[512,1024]{1,0:T(8,128)(2,1)}, bf16[512,1024]{1,0:T(8,128)(2,1)S(1)}, u32[]{:S(2)}, u32[]{:S(2)}) collective-permute-start(bf16[512,1024]{1,0:T(8,128)(2,1)} %param.8), channel_id=1, source_target_pairs={{0,20},{4,24},{8,28},{12,0},{16,4},{20,8},{24,12},{28,16},{1,21},{... | collective-permute-start | bytes 3145736 | tf_op jit(solution)/shard_map/ppermute | solution.py:15
  12.3 1.3 collective-permute-start.1
  14.2 1.4 fusion.12
  15.6 2.1 pad_add_fusion.1
  17.6 0.7 fusion.15
  18.9 0.7 broadcast_select_fusion.2
  19.6 16.6 %collective-permute-done.2 = bf16[512,1024]{1,0:T(8,128)(2,1)S(1)} collective-permute-done((bf16[512,1024]{1,0:T(8,128)(2,1)}, bf16[512,1024]{1,0:T(8,128)(2,1)S(1)}, u32[]{:S(2)}, u32[]{:S(2)}) %collective-permute-start.2) | collective-permute-done | bytes 1048608 | tf_op jit(solution)/shard_map/ppermute | solution.py:15
  36.2 23.7 %collective-permute-done.1 = bf16[512,1024]{1,0:T(8,128)(2,1)S(1)} collective-permute-done((bf16[512,1024]{1,0:T(8,128)(2,1)}, bf16[512,1024]{1,0:T(8,128)(2,1)S(1)}, u32[]{:S(2)}, u32[]{:S(2)}) %collective-permute-start.1) | collective-permute-done | bytes 1048608 | tf_op jit(solution)/shard_map/ppermute | solution.py:15
  59.9 20.1 %collective-permute-done = bf16[512,1024]{1,0:T(8,128)(2,1)} collective-permute-done((bf16[512,1024]{1,0:T(8,128)(2,1)}, bf16[512,1024]{1,0:T(8,128)(2,1)}, u32[]{:S(2)}, u32[]{:S(2)}) %collective-permute-start) | collective-permute-done | bytes 1048608 | tf_op jit(solution)/shard_map/ppermute | solution.py:15
  80.0 3.2 pad_maximum_fusion.1
  83.2 4.4 %gather_fusion.1 = bf16[3,512,1024]{2,1,0:T(8,128)(2,1)} fusion(bf16[3,512,1024]{2,1,0:T(8,128)(2,1)} %pad_maximum_fusion.1, s32[1024]{0:T(1024)S(1)} %pad_clamp_fusion), kind=kCustom, calls=%fused_computation.1 | custom fusion | bytes 6291468 | tf_op jit(solution)/shard_map/jit(_take)/gather | solution.py:38
  87.7 2.3 broadcast_select_fusion
  90.0 1.7 copy-done.1
  91.7 4.3 %fusion.2 = f32[4,512,512]{1,2,0:T(8,128)} fusion(bf16[3,512,1024]{2,1,0:T(8,128)(2,1)S(1)} %broadcast_select_fusion, bf16[1,512,1024]{2,1,0:T(8,128)(2,1)S(1)} %bitcast.50, bf16[512,1024]{1,0:T(8,128)(2,1)S(1)} %copy-done), kind=kOutput, calls=%fused_computation.12 | convolution fusion | flops 2149580800 | bytes 9437184 | tf_op jit(solution)/shard_map/id,kjd->kij/dot_general | solution.py:45
  96.7 3.3 collective-permute-start.5
  100.0 23.8 %collective-permute-start.4 = (bf16[512]{0:T(512)(128)(2,1)S(1)}, bf16[512]{0:T(512)(128)(2,1)S(1)}, u32[]{:S(2)}, u32[]{:S(2)}) collective-permute-start(bf16[512]{0:T(512)(128)(2,1)S(1)} %copy-done.3), channel_id=1, source_target_pairs={{0,24},{4,28},{8,0},{12,4},{16,8},{20,12},{24,16},{28,20},{1,25},{... | collective-permute-start | bytes 3080 | tf_op jit(solution)/shard_map/ppermute | solution.py:15
  124.5 0.7 pad_add_fusion.2
  125.5 0.9 collective-permute-done.4
  126.4 1.0 collective-permute-done.3
  128.1 36.8 %reduce-scatter.2.cloned.1.call-done = f32[4,128,512]{1,2,0:T(8,128)} async-done(((f32[4,512,512]{1,2,0:T(8,128)}), f32[4,128,512]{1,2,0:T(8,128)}) %reduce-scatter.2.cloned.1.call-update) | async-done | bytes 1048592 | tf_op jit(solution)/shard_map/reduce_scatter | solution.py:48
  164.8 1.8 select_reduce_fusion.3
  167.6 1.3 convert_reduce_fusion
  168.9 1.3 multiply_convert_fusion
  170.3 0.7 all-gather.3.cloned.1.call-update
  171.0 22.2 %all-gather.5.cloned.1.call-done = bf16[4,512,512]{1,2,0:T(8,128)(2,1)} async-done(((bf16[4,128,512]{1,2,0:T(8,128)(2,1)}), bf16[4,512,512]{1,2,0:T(8,128)(2,1)}) %all-gather.5.cloned.1.call-update) | async-done | bytes 2097168 | tf_op jit(solution)/shard_map/all_gather | solution.py:72
  193.2 5.5 %select_reduce_fusion.2 = (bf16[512,1024]{1,0:T(8,128)(2,1)S(1)}, bf16[512,1024]{1,0:T(8,128)(2,1)}, bf16[512,1024]{1,0:T(8,128)(2,1)}) fusion(pred[3]{0:T(512)(128)(4,1)S(1)} %get-tuple-element.24, pred[3]{0:T(512)(128)(4,1)S(1)} %get-tuple-element.26, pred[3]{0:T(512)(128)(4,1)S(1)} %get-tuple-element.23, ...), kind=kOutput, calls=%fused_computation.7 | convolution fusion | flops 1620049920 | bytes 6291465 | tf_op jit(solution)/shard_map/kij,id->kjd/dot_general | solution.py:79
  198.6 2.4 collective-permute-start.8
  201.0 1.5 collective-permute-start.7
  202.5 1.5 collective-permute-start.6
  204.0 112.5 %all-reduce = (f32[]{:T(128)}, f32[]{:T(128)}) all-reduce(f32[]{:T(128)} %get-tuple-element.7, f32[]{:T(128)} %get-tuple-element.6), channel_id=1, replica_groups=mesh['dp'=8,'mp'=4] {'dp','mp'}, use_global_device_ids=true, to_apply=%region_9.10 | all-reduce | flops 2 | bytes 16 | tf_op jit(solution)/shard_map/psum | solution.py:74
  317.9 5.9 %bitcast_convert_fusion = bf16[512,1024]{1,0:T(8,128)(2,1)} fusion(bf16[4,512,512]{1,2,0:T(8,128)(2,1)} %all-gather.3.cloned.1.call-done, bf16[3,512,1024]{2,1,0:T(8,128)(2,1)} %copy-done.1, bf16[1,512,1024]{2,1,0:T(8,128)(2,1)S(1)} %bitcast.51), kind=kOutput, calls=%fused_computation.13 | convolution fusion | flops 2150105088 | bytes 7340032 | tf_op jit(solution)/shard_map/kij,kjd->id/dot_general | solution.py:75
  323.7 3.9 %add_convert_fusion = bf16[512,1024]{1,0:T(8,128)(2,1)} fusion(bf16[512,1024]{1,0:T(8,128)(2,1)} %collective-permute-done.8, bf16[512,1024]{1,0:T(8,128)(2,1)} %collective-permute-done.7, bf16[512,1024]{1,0:T(8,128)(2,1)} %collective-permute-done.6, bf16[512,1024]{1,0:T(8,128)(2,1)S(1)} %copy-done, bf16[4,512,512]{1,2,0:T(8,128)(2,1)} %all-gather.5.cloned.1.call-done), kind=kOutput, calls=%fused_computation.14 | convolution fusion | flops 540540928 | bytes 5767168 | tf_op jit(solution)/shard_map/ij,id->jd/dot_general | solution.py:78
  (43 shorter events, 4.6 us)
Async XLA Ops:
  7.2 84.6 %copy-start = (bf16[512,1024]{1,0:T(8,128)(2,1)S(1)}, bf16[512,1024]{1,0:T(8,128)(2,1)}, u32[]{:S(2)}) copy-start(bf16[512,1024]{1,0:T(8,128)(2,1)} %param.7) | copy-start | bytes 3145732
  7.2 157.7 %reduce-scatter.2.cloned.1.call-start = ((), (), s32[]{:S(2)}) async-start(), calls=%async_computation.1 | async-start | bytes 5242880 | tf_op jit(solution)/shard_map/reduce_scatter | solution.py:48
  7.2 29.0 %collective-permute-start.2 = (bf16[512,1024]{1,0:T(8,128)(2,1)}, bf16[512,1024]{1,0:T(8,128)(2,1)S(1)}, u32[]{:S(2)}, u32[]{:S(2)}) collective-permute-start(bf16[512,1024]{1,0:T(8,128)(2,1)} %param.8), channel_id=1, source_target_pairs={{0,20},{4,24},{8,28},{12,0},{16,4},{20,8},{24,12},{28,16},{1,21},{... | collective-permute-start | bytes 3145736 | tf_op jit(solution)/shard_map/ppermute | solution.py:15
  12.3 47.6 %collective-permute-start.1 = (bf16[512,1024]{1,0:T(8,128)(2,1)}, bf16[512,1024]{1,0:T(8,128)(2,1)S(1)}, u32[]{:S(2)}, u32[]{:S(2)}) collective-permute-start(bf16[512,1024]{1,0:T(8,128)(2,1)} %param.8), channel_id=1, source_target_pairs={{0,24},{4,28},{8,0},{12,4},{16,8},{20,12},{24,16},{28,20},{1,25},{... | collective-permute-start | bytes 3145736 | tf_op jit(solution)/shard_map/ppermute | solution.py:15
  13.6 66.4 %collective-permute-start = (bf16[512,1024]{1,0:T(8,128)(2,1)}, bf16[512,1024]{1,0:T(8,128)(2,1)}, u32[]{:S(2)}, u32[]{:S(2)}) collective-permute-start(bf16[512,1024]{1,0:T(8,128)(2,1)} %param.8), channel_id=1, source_target_pairs={{0,28},{4,0},{8,4},{12,8},{16,12},{20,16},{24,20},{28,24},{1,29},{... | collective-permute-start | bytes 3145736 | tf_op jit(solution)/shard_map/ppermute | solution.py:15
  87.7 4.0 %copy-start.5 = (bf16[512,1024]{1,0:T(8,128)(2,1)S(1)}, bf16[512,1024]{1,0:T(8,128)(2,1)}, u32[]{:S(2)}) copy-start(bf16[512,1024]{1,0:T(8,128)(2,1)} %param.8) | copy-start | bytes 3145732
  90.0 1.7 copy-start.1
  96.0 0.7 copy-start.3
  96.0 29.1 %copy-start.2 = (s32[1,3]{1,0:T(1,128)S(1)}, s32[1,3]{1,0:T(1,128)}, u32[]{:S(2)}) copy-start(s32[1,3]{1,0:T(1,128)} %param.11) | copy-start | bytes 40
  96.0 29.2 %copy-start.4 = (bf16[512]{0:T(512)(128)(2,1)S(1)}, bf16[512]{0:T(512)(128)(2,1)}, u32[]{:S(2)}) copy-start(bf16[512]{0:T(512)(128)(2,1)} %param.9) | copy-start | bytes 3076
  96.1 97.1 %all-gather.5.cloned.1.call-start = ((), (), s32[]{:S(2)}) async-start(), calls=%async_computation.3 | async-start | bytes 2621440 | tf_op jit(solution)/shard_map/all_gather | solution.py:72
  96.7 28.7 %collective-permute-start.5 = (bf16[512]{0:T(512)(128)(2,1)S(1)}, bf16[512]{0:T(512)(128)(2,1)S(1)}, u32[]{:S(2)}, u32[]{:S(2)}) collective-permute-start(bf16[512]{0:T(512)(128)(2,1)S(1)} %copy-done.3), channel_id=1, source_target_pairs={{0,20},{4,24},{8,28},{12,0},{16,4},{20,8},{24,12},{28,16},{1,21},{... | collective-permute-start | bytes 3080 | tf_op jit(solution)/shard_map/ppermute | solution.py:15
  100.0 26.4 %collective-permute-start.4 = (bf16[512]{0:T(512)(128)(2,1)S(1)}, bf16[512]{0:T(512)(128)(2,1)S(1)}, u32[]{:S(2)}, u32[]{:S(2)}) collective-permute-start(bf16[512]{0:T(512)(128)(2,1)S(1)} %copy-done.3), channel_id=1, source_target_pairs={{0,24},{4,28},{8,0},{12,4},{16,8},{20,12},{24,16},{28,20},{1,25},{... | collective-permute-start | bytes 3080 | tf_op jit(solution)/shard_map/ppermute | solution.py:15
  123.8 3.6 %collective-permute-start.3 = (bf16[512]{0:T(512)(128)(2,1)S(1)}, bf16[512]{0:T(512)(128)(2,1)S(1)}, u32[]{:S(2)}, u32[]{:S(2)}) collective-permute-start(bf16[512]{0:T(512)(128)(2,1)S(1)} %copy-done.3), channel_id=1, source_target_pairs={{0,28},{4,0},{8,4},{12,8},{16,12},{20,16},{24,20},{28,24},{1,29},{... | collective-permute-start | bytes 3080 | tf_op jit(solution)/shard_map/ppermute | solution.py:15
  170.2 147.7 %all-gather.3.cloned.1.call-start = ((), (), s32[]{:S(2)}) async-start(), calls=%async_computation.2 | async-start | bytes 2621440 | tf_op jit(solution)/shard_map/all_gather | solution.py:71
  198.6 125.1 %collective-permute-start.8 = (bf16[512,1024]{1,0:T(8,128)(2,1)}, bf16[512,1024]{1,0:T(8,128)(2,1)}, u32[]{:S(2)}, u32[]{:S(2)}) collective-permute-start(bf16[512,1024]{1,0:T(8,128)(2,1)} %get-tuple-element.4), channel_id=1, source_target_pairs={{0,12},{4,16},{8,20},{12,24},{16,28},{20,0},{24,4},{28,8},{1,13},{... | collective-permute-start | bytes 3145736 | tf_op jit(solution)/shard_map/ppermute | solution.py:15
  201.0 122.7 %collective-permute-start.7 = (bf16[512,1024]{1,0:T(8,128)(2,1)}, bf16[512,1024]{1,0:T(8,128)(2,1)}, u32[]{:S(2)}, u32[]{:S(2)}) collective-permute-start(bf16[512,1024]{1,0:T(8,128)(2,1)} %get-tuple-element.5), channel_id=1, source_target_pairs={{0,8},{4,12},{8,16},{12,20},{16,24},{20,28},{24,0},{28,4},{1,9},{5... | collective-permute-start | bytes 3145736 | tf_op jit(solution)/shard_map/ppermute | solution.py:15
  202.5 121.2 %collective-permute-start.6 = (bf16[512,1024]{1,0:T(8,128)(2,1)S(1)}, bf16[512,1024]{1,0:T(8,128)(2,1)}, u32[]{:S(2)}, u32[]{:S(2)}) collective-permute-start(bf16[512,1024]{1,0:T(8,128)(2,1)S(1)} %get-tuple-element.3), channel_id=1, source_target_pairs={{0,4},{4,8},{8,12},{12,16},{16,20},{20,24},{24,28},{28,0},{1,5},{5... | collective-permute-start | bytes 3145736 | tf_op jit(solution)/shard_map/ppermute | solution.py:15
Sparse Core Ops, SparseCore 0:
  96.2 68.6 reduce-scatter.1
  170.3 22.7 all-gather.4
  195.3 23.1 all-gather.2
where the time goes:
time: 336 us; the launch traced here: 335 us
  waiting for transfers between devices  122 us (36%)
  blocking collectives  112 us (33%)
  starting transfers between devices  40.1 us (12%)
  matrix products  19.5 us (6%)
  other arithmetic  16.7 us (5%)
  between operations  16.3 us (5%)
  local copies, waits for them, and re-layouts  8.01 us (2%)
    psum x1, blocking collectives, local(): loss_all, valid_all = lax.psum((loss_sum, valid_sum), ('dp', 'mp'))  112 us
    ppermute x9, waiting for transfers between devices, shifted(): return lax.ppermute(value, axis, pairs)  62.3 us
    ppermute x9, starting transfers between devices, shifted(): return lax.ppermute(value, axis, pairs)  40 us
    reduce_scatter x1, waiting for transfers between devices, local(): summed = lax.psum_scatter(raw, 'mp', scatter_dimension=1, tiled=True)  36.8 us
    all_gather x1, waiting for transfers between devices, local(): lax.all_gather(row_weight, 'mp', axis=1, tiled=True)  22.2 us
  transfers between devices with their start and end apart: 12, of which 7 were waited for; matrix products, arithmetic and copies ran while one was open for 5% of the time, Pallas kernels for 0%

commit v1 on v0

v1 whole, which is shorter than its diff:
```python
import functools
import math

import jax
import jax.numpy as jnp
from jax import lax
from jax.experimental import pallas as pl
from jax.experimental.pallas import tpu as pltpu
from jax.sharding import PartitionSpec as P

WIN = 3
CHUNKS = 4
GROUP = 32
MESH = pl.DeviceIdType.MESH


def kernel(ndp, nmp, inv, q_ref, p_ref, ps_ref, qs_ref, ok_ref, bias_ref,
           gq_ref, gp_ref, loss_ref,
           pbuf, qbuf, psbuf, raw, inbox, weights, rw_out, rw_in, acc, lsum, lin,
           p_ss, p_rs, q_ss, q_rs, sc_ss, sc_rs, t_ss, t_rs, k_ss, k_rs,
           d_ss, d_rs, g_ss, g_rs, l_ss, l_rs):
    d = lax.axis_index("dp")
    m = lax.axis_index("mp")
    rows, width = q_ref.shape
    share = rows // nmp
    step = rows // CHUNKS

    def at_dp(delta):
        return (lax.rem(d + delta + ndp, ndp), m)

    def at_mp(delta):
        return (d, lax.rem(m + delta, nmp))

    def flip(index, bit):
        return index + bit - 2 * bit * lax.rem(index // bit, 2)

    def rows_of(block):
        return pl.ds(pl.multiple_of(block * share, share), share)

    even = lax.rem(d, 2) == 0
    odd = lax.rem(d, 2) == 1
    partner = (flip(d, 1), m)
    mp_bits = [1 << b for b in range(nmp.bit_length() - 1)]
    dp_bits = [1 << b for b in range(ndp.bit_length() - 1)]

    peers = [at_dp(s * k) for k in range(1, WIN + 1) for s in (1, -1)]
    peers += [at_mp(j) for j in range(1, nmp)]
    peers += [(flip(d, b), m) for b in dp_bits if b > WIN]
    barrier = pltpu.get_barrier_semaphore()
    for peer in peers:
        pl.semaphore_signal(barrier, inc=1, device_id=peer, device_id_type=MESH)
    pl.semaphore_wait(barrier, len(peers))

    def copy(src, dst, ssem, rsem, dev):
        return pltpu.make_async_remote_copy(
            src_ref=src, dst_ref=dst, send_sem=ssem, recv_sem=rsem,
            device_id=dev, device_id_type=MESH)

    class Stream:
        def __init__(self, own, buf, ss, rs, dest):
            self.own, self.buf, self.ss, self.rs, self.dest = own, buf, ss, rs, dest

        def cut(self, c):
            return pl.ds(c * step, step)

        def direct(self, c):
            s = self.cut(c)
            return copy(self.own.at[s], self.buf.at[1, s], self.ss.at[0, c], self.rs.at[1, c], self.dest)

        def near_relay(self, c):
            s = self.cut(c)
            return copy(self.buf.at[1, s], self.buf.at[0, s], self.ss.at[1, c], self.rs.at[0, c], partner)

        def near_own(self, c):
            s = self.cut(c)
            return copy(self.own.at[s], self.buf.at[0, s], self.ss.at[1, c], self.rs.at[0, c], partner)

        def far_near(self, c):
            s = self.cut(c)
            return copy(self.buf.at[1, s], self.buf.at[2, s], self.ss.at[2, c], self.rs.at[2, c], partner)

        def far_next(self, c):
            s = self.cut(c)
            return copy(self.buf.at[0, s], self.buf.at[2, s], self.ss.at[3, c], self.rs.at[2, c], self.dest)

        def arrived(self, slot, c):
            s = self.cut(c)
            copy(self.buf.at[slot, s], self.buf.at[slot, s], self.ss.at[0, c], self.rs.at[slot, c], partner).wait_recv()

        def start_own(self, is_b):
            for c in range(CHUNKS):
                self.direct(c).start()

            @pl.when(is_b)
            def _():
                for c in range(CHUNKS):
                    self.near_own(c).start()

        def relay_two(self, is_b):
            for c in range(CHUNKS):
                self.arrived(1, c)

                @pl.when(is_b)
                def _():
                    self.far_near(c).start()

                @pl.when(jnp.logical_not(is_b))
                def _():
                    self.near_relay(c).start()

        def relay_one(self, is_b):
            for c in range(CHUNKS):
                self.arrived(0, c)

                @pl.when(is_b)
                def _():
                    self.far_next(c).start()

        def relay_all(self, is_b):
            for c in range(CHUNKS):
                self.arrived(1, c)

                @pl.when(is_b)
                def _():
                    self.far_near(c).start()
                    self.arrived(0, c)
                    self.far_next(c).start()

                @pl.when(jnp.logical_not(is_b))
                def _():
                    self.near_relay(c).start()
                    self.arrived(0, c)

        def finish(self, is_b):
            for c in range(CHUNKS):
                self.direct(c).wait_send()

                @pl.when(is_b)
                def _():
                    self.near_own(c).wait_send()
                    self.far_near(c).wait_send()
                    self.far_next(c).wait_send()

                @pl.when(jnp.logical_not(is_b))
                def _():
                    self.near_relay(c).wait_send()

    ps = Stream(p_ref, pbuf, p_ss, p_rs, at_dp(-2))
    qs = Stream(q_ref, qbuf, q_ss, q_rs, at_dp(2))

    def scale_copy(k):
        return copy(ps_ref, psbuf.at[k - 1], sc_ss.at[k - 1], sc_rs.at[k - 1], at_dp(-k))

    for k in range(1, WIN + 1):
        scale_copy(k).start()
    ps.start_own(odd)

    def tile_copy(k, j):
        return copy(raw.at[k, rows_of(lax.rem(m + j, nmp))], inbox.at[j - 1, k],
                    t_ss.at[j - 1, k], t_rs.at[j - 1, k], at_mp(j))

    def tile(k):
        keys = p_ref if k == 0 else pbuf.at[k - 1]

        @pl.loop(0, nmp)
        def _(r):
            at = rows_of(r)
            raw[k, at, :] = lax.dot_general(
                q_ref[at, :], keys[...], (((1,), (1,)), ((), ())),
                preferred_element_type=jnp.float32)
        for j in range(1, nmp):
            tile_copy(k, j).start()

    tile(0)
    ps.relay_two(odd)
    qs.start_own(even)
    ps.relay_one(odd)
    tile(2)
    tile(1)
    qs.relay_two(even)
    for c in range(CHUNKS):
        ps.arrived(2, c)
    tile(3)
    for k in range(1, WIN + 1):
        scale_copy(k).wait_recv()
    for k in (0, 2, 1, 3):
        for j in range(1, nmp):
            tile_copy(k, j).wait_recv()

    lsum[...] = jnp.zeros_like(lsum)

    @pl.loop(0, share // GROUP)
    def _(g):
        low = pl.multiple_of(g * GROUP, GROUP)
        here = pl.ds(low, GROUP)
        whole = pl.ds(pl.multiple_of(m * share + low, GROUP), GROUP)
        row_scale = qs_ref[whole, :]
        valid = ok_ref[whole, :] > 0.0
        cols = lax.broadcasted_iota(jnp.int32, (GROUP, rows), 1)
        ids = lax.broadcasted_iota(jnp.int32, (GROUP, rows), 0) + (m * share + low)
        diagonal = cols == ids
        key_scale = [ps_ref[0:1, :]] + [psbuf[k, 0:1, :] for k in range(WIN)]
        scores = []
        for k in range(WIN + 1):
            s = raw[k, whole, :]
            for j in range(nmp - 1):
                s = s + inbox[j, k, here, :]
            scores.append(s * (row_scale * inv) * key_scale[k])
        masked = [scores[k] + bias_ref[k:k + 1, :] for k in range(WIN + 1)]
        top = functools.reduce(jnp.maximum, [jnp.max(x, axis=1, keepdims=True) for x in masked])
        exps = [jnp.exp(x - top) for x in masked]
        total = sum(jnp.sum(x, axis=1, keepdims=True) for x in exps)
        lse = top + jnp.log(total)
        positive = jnp.sum(jnp.where(diagonal, scores[0], 0.0), axis=1, keepdims=True)
        lost = jnp.sum(jnp.where(valid, lse - positive, 0.0), axis=0, keepdims=True)
        lsum[0] = lsum[0] + lost
        for k in range(WIN + 1):
            grad = exps[k] / total
            if k == 0:
                grad = grad - diagonal.astype(jnp.float32)
            grad = jnp.where(valid, grad, 0.0)
            weights[k, whole, :] = (grad * key_scale[k]).astype(jnp.bfloat16)
            if k == 0:
                weights[WIN + 1, whole, :] = (grad * row_scale).astype(jnp.bfloat16)
            else:
                rw_out[k - 1, here, :] = (grad * row_scale).astype(jnp.bfloat16)

    def dispatch(k):
        return copy(rw_out.at[k - 1], rw_in.at[k - 1, rows_of(m)], d_ss.at[k - 1], d_rs.at[k - 1], at_dp(k))

    for k in range(1, WIN + 1):
        dispatch(k).start()

    class Gather:
        def __init__(self, buf, ss, rs):
            self.buf, self.ss, self.rs = buf, ss, rs
            known = [0]
            self.steps = []
            for bit in reversed(mp_bits):
                self.steps += [(s, bit) for s in known]
                known = known + [s ^ bit for s in known]
            self.steps.sort(key=lambda t: t[0])
            self.got = set()

        def hop(self, s, bit):
            block = m
            for b in mp_bits:
                if s & b:
                    block = flip(block, b)
            part = self.buf.at[:, rows_of(block)]
            return copy(part, part, self.ss.at[s ^ bit], self.rs.at[s ^ bit], (d, flip(m, bit)))

        def take(self, s):
            if s and s not in self.got:
                self.got.add(s)
                block = m
                for b in mp_bits:
                    if s & b:
                        block = flip(block, b)
                part = self.buf.at[:, rows_of(block)]
                copy(part, part, self.ss.at[s], self.rs.at[s], (d, flip(m, 1))).wait_recv()

        def begin(self):
            for s, bit in self.steps:
                if s == 0:
                    self.hop(s, bit).start()

        def rest(self):
            for s, bit in self.steps:
                if s:
                    self.take(s)
                    self.hop(s, bit).start()

        def all(self):
            for s in range(1, nmp):
                self.take(s)

        def finish(self):
            for s, bit in self.steps:
                self.hop(s, bit).wait_send()

    local = Gather(weights, k_ss, k_rs)
    foreign = Gather(rw_in, g_ss, g_rs)
    local.begin()
    qs.relay_one(even)
    for k in range(1, WIN + 1):
        dispatch(k).wait_recv()
    foreign.begin()
    local.rest()
    local.all()
    foreign.rest()

    @pl.loop(0, nmp)
    def _(r):
        at = rows_of(r)
        out = jnp.dot(weights[0, at, :], p_ref[...], preferred_element_type=jnp.float32)
        for k in range(WIN):
            out = out + jnp.dot(weights[k + 1, at, :], pbuf[k], preferred_element_type=jnp.float32)
        gq_ref[at, :] = out.astype(jnp.bfloat16)

    def back(w, x):
        return lax.dot_general(w, x, (((0,), (0,)), ((), ())), preferred_element_type=jnp.float32)

    stages = [(d, flip(m, b)) for b in mp_bits] + [(flip(d, b), m) for b in dp_bits]

    def loss_copy(i):
        return copy(lsum.at[i], lin.at[i], l_ss.at[i], l_rs.at[i], stages[i])

    for i in range(len(stages)):
        loss_copy(i).start()
        loss_copy(i).wait_recv()
        lsum[i + 1] = lsum[i] + lin[i]
    loss_ref[...] = lsum[len(stages)]

    for c in range(CHUNKS):
        qs.arrived(2, c)
    foreign.all()
    jc = 128

    @pl.loop(0, rows // jc)
    def _(t):
        at = pl.ds(pl.multiple_of(t * jc, jc), jc)
        out = back(weights[WIN + 1, :, at], q_ref[...])
        for k in range(WIN):
            out = out + back(rw_in[k, :, at], qbuf[k])
        gp_ref[at, :] = out.astype(jnp.bfloat16)

    ps.finish(odd)
    qs.finish(even)
    for k in range(1, WIN + 1):
        scale_copy(k).wait_send()
        dispatch(k).wait_send()
    for k in range(WIN + 1):
        for j in range(1, nmp):
            tile_copy(k, j).wait_send()
    local.finish()
    foreign.finish()
    for i in range(len(stages)):
        loss_copy(i).wait_send()


def local(ndp, nmp, query, passage, query_scale, passage_scale, partners, counts):
    rows, width = query.shape
    inv = 1.0 / math.sqrt(width * nmp)
    share = rows // nmp
    mine = lax.axis_index("dp")
    ids = jnp.arange(counts.shape[0], dtype=jnp.int32)
    offsets = jnp.arange(WIN + 1, dtype=jnp.int32)
    near = (mine + offsets) % ndp
    key_counts = jnp.sum(jnp.where(ids[None, :] == near[:, None], counts[None, :], 0), axis=1)
    live = (offsets == 0) | jnp.any(partners[0][None, :] == offsets[:, None], axis=1)
    column = jnp.arange(rows, dtype=jnp.int32)
    bias = jnp.where(live[:, None] & (column[None, :] < key_counts[:, None]), 0.0, -jnp.inf).astype(jnp.float32)
    ok = (column < key_counts[0]).astype(jnp.float32)[:, None]
    ps = jnp.broadcast_to(passage_scale.astype(jnp.float32)[None, :], (8, rows))
    qs = query_scale.astype(jnp.float32)[:, None]
    nst = (ndp * nmp).bit_length() - 1
    bf, f32 = jnp.bfloat16, jnp.float32
    dma = pltpu.SemaphoreType.DMA
    vm = pl.BlockSpec(memory_space=pltpu.VMEM)
    gq, gp, loss = pl.pallas_call(
        functools.partial(kernel, ndp, nmp, inv),
        out_shape=[
            jax.ShapeDtypeStruct((rows, width), bf),
            jax.ShapeDtypeStruct((rows, width), bf),
            jax.ShapeDtypeStruct((8, 128), f32),
        ],
        in_specs=[vm] * 6,
        out_specs=[vm] * 3,
        scratch_shapes=[
            pltpu.VMEM((WIN, rows, width), bf),
            pltpu.VMEM((WIN, rows, width), bf),
            pltpu.VMEM((WIN, 8, rows), f32),
            pltpu.VMEM((WIN + 1, rows, rows), f32),
            pltpu.VMEM((nmp - 1, WIN + 1, share, rows), f32),
            pltpu.VMEM((WIN + 2, rows, rows), bf),
            pltpu.VMEM((WIN, share, rows), bf),
            pltpu.VMEM((WIN, rows, rows), bf),
            pltpu.VMEM((8, 128), f32),
            pltpu.VMEM((nst + 1, 8, 128), f32),
            pltpu.VMEM((nst, 8, 128), f32),
            dma((4, CHUNKS)), dma((WIN, CHUNKS)),
            dma((4, CHUNKS)), dma((WIN, CHUNKS)),
            dma((WIN,)), dma((WIN,)),
            dma((nmp - 1, WIN + 1)), dma((nmp - 1, WIN + 1)),
            dma((nmp,)), dma((nmp,)),
            dma((WIN,)), dma((WIN,)),
            dma((nmp,)), dma((nmp,)),
            dma((nst,)), dma((nst,)),
        ],
        compiler_params=pltpu.CompilerParams(
            collective_id=0, has_side_effects=True, vmem_limit_bytes=56 * 1024 * 1024),
    )(query, passage, ps, qs, ok, bias)
    return loss[0, 0] / jnp.sum(counts).astype(f32), gq, gp


def solution(mesh):
    return jax.shard_map(
        functools.partial(local, mesh.shape["dp"], mesh.shape["mp"]),
        mesh=mesh,
        in_specs=(P("dp", "mp"), P("dp", "mp"), P("dp"), P("dp"), P("dp", None), P()),
        out_specs=(P(), P("dp", "mp"), P("dp", "mp")),
        check_vma=False,
    )
```

time: 336 us -> 149 us (0.44)
  Pallas kernels: 0 us -> 135 us
  waiting for transfers between devices: 122 us -> 0 us
  blocking collectives: 112 us -> 0 us
  starting transfers between devices: 40.1 us -> 0 us
  matrix products: 19.5 us -> 0 us
  other arithmetic: 16.7 us -> 2.38 us
  between operations: 16.3 us -> 3.12 us
    pallas_call x0 -> x1, Pallas kernels: none -> 135 us  [local(): pl.pallas_call(functools.partial(kernel, ndp, nmp, inv), out_shape=[jax.S...]
    psum x1 -> x0, blocking collectives: 112 us -> none  [local(): loss_all, valid_all = lax.psum((loss_sum, valid_sum), ('dp', 'mp'))]
    ppermute x9 -> x0, waiting for transfers between devices: 62.3 us -> none  [shifted(): return lax.ppermute(value, axis, pairs)]
    ppermute x9 -> x0, starting transfers between devices: 40 us -> none  [shifted(): return lax.ppermute(value, axis, pairs)]
    reduce_scatter x1 -> x0, waiting for transfers between devices: 36.8 us -> none  [local(): summed = lax.psum_scatter(raw, 'mp', scatter_dimension=1, tiled=True)]
    all_gather x2 -> x0, waiting for transfers between devices: 22.2 us -> none  [the longest x1 22.2 us: local(): lax.all_gather(row_weight, 'mp', axis=1, tiled=True)]
    dot_general x4 -> x0, matrix products: 19.5 us -> none  [the longest x1 5.86 us: local(): jnp.einsum('kij,kjd->id', key_weight, keys, preferred_element_type=jnp.fl...]
    gather x3 -> x0, local copies, waits for them, and re-layouts: 5.64 us -> none  [the longest x1 4.44 us: local(): jnp.take(jnp.stack(far_rows), pick, axis=0)]
  transfers between devices with their start and end apart: 12 -> 0, of which waited for: 7 -> 0; matrix products, arithmetic and copies ran while one was open for 5% -> 0% of each run, Pallas kernels for 0% -> 0%
where the time goes in v1:
time: 149 us
  Pallas kernels  135 us (91%)
  local copies, waits for them, and re-layouts  7.96 us (5%)
  between operations  3.12 us (2%)
  other arithmetic  2.38 us (2%)
    pallas_call x1, Pallas kernels, local(): pl.pallas_call(functools.partial(kernel, ndp, nmp, inv), out_shape=[jax.S...  135 us
    unnamed x12, local copies, waits for them, and re-layouts  5.31 us

profile of v1, /device:TPU:0, one launch (start us, length us, event | category | flops | bytes accessed | tf_op | source)
XLA Modules:
  0.0 148.6 jit_solution(13294793040513384937)
XLA Ops:
  0.6 0.0 copy-start.3
  0.6 0.6 copy-done.3
  1.3 0.6 reduce_sum.19
  2.6 0.2 select_reduce_fusion
  2.8 0.0 copy-start.4
  2.8 0.7 copy-done.4
  3.4 0.1 fusion.3
  3.6 0.0 copy-start.1
  3.6 0.7 copy-done.1
  4.2 0.0 copy-start.2
  4.2 0.7 fusion.2.bias_ref
  4.9 0.0 copy-done.2
  4.9 0.6 broadcast_in_dim.39.ps_ref
  5.5 0.9 copy.10.qs_ref
  6.4 0.8 fusion.ok_ref
  7.1 135.1 %shard_map.85 = (bf16[512,1024]{1,0:T(8,128)(2,1)}, bf16[512,1024]{1,0:T(8,128)(2,1)}, f32[8,128]{1,0:T(8,128)}) custom-call(bf16[512,1024]{1,0:T(8,128)(2,1)} %q_ref.1, bf16[512,1024]{1,0:T(8,128)(2,1)} %p_ref.1, f32[8,512]{1,0:T(8,128)} %broadcast_in_dim.39.ps_ref, f32[512,1]{1,0:T(8,128)} %copy.10.qs_ref, f32[512,1]{1,0:T(8,128)} %fusion.ok_ref, ...), custom_call_target="tpu_custom_call" | custom-call | tf_op jit(solution)/shard_map/pallas_call | solution.py:361
  142.3 1.2 slice.7
  144.1 0.0 copy-start
  144.1 2.4 %copy.13 = bf16[512,1024]{1,0:T(8,128)(2,1)} copy(bf16[512,1024]{1,0:T(8,128)(2,1)} %get-tuple-element.13) | data formatting | bytes 2097152
  146.5 0.0 copy-done
  146.5 1.0 copy.14
  (3 shorter events, 0.0 us)
Async XLA Ops:
  0.6 0.7 copy-start.3
  2.8 0.7 copy-start.4
  3.6 0.7 copy-start.1
  4.2 0.7 copy-start.2
  144.1 2.4 %copy-start = (bf16[512,1024]{1,0:T(8,128)(2,1)S(1)}, bf16[512,1024]{1,0:T(8,128)(2,1)}, u32[]{:S(2)}) copy-start(bf16[512,1024]{1,0:T(8,128)(2,1)} %get-tuple-element.14) | copy-start | bytes 3145732

commit v2 on v1

--- a/solution.py
+++ b/solution.py
@@ -14,9 +14,9 @@
 MESH = pl.DeviceIdType.MESH
 
 
-def kernel(ndp, nmp, inv, q_ref, p_ref, ps_ref, qs_ref, ok_ref, bias_ref,
+def kernel(ndp, nmp, inv, q_ref, p_ref, ps_ref, qs_ref, meta_ref,
            gq_ref, gp_ref, loss_ref,
-           pbuf, qbuf, psbuf, raw, inbox, weights, rw_out, rw_in, acc, lsum, lin,
+           pbuf, qbuf, psbuf, raw, inbox, weights, rw_out, rw_in, lsum, lin,
            p_ss, p_rs, q_ss, q_rs, sc_ss, sc_rs, t_ss, t_rs, k_ss, k_rs,
            d_ss, d_rs, g_ss, g_rs, l_ss, l_rs):
     d = lax.axis_index("dp")
@@ -155,9 +155,25 @@
         scale_copy(k).start()
     ps.start_own(odd)
 
-    def tile_copy(k, j):
-        return copy(raw.at[k, rows_of(lax.rem(m + j, nmp))], inbox.at[j - 1, k],
-                    t_ss.at[j - 1, k], t_rs.at[j - 1, k], at_mp(j))
+    def across(s):
+        block = m
+        for b in mp_bits:
+            if s & b:
+                block = flip(block, b)
+        return rows_of(block)
+
+    def tile_copy(k, s):
+        return copy(raw.at[k, across(s)], inbox.at[s - 1, k],
+                    t_ss.at[s - 1, k], t_rs.at[s - 1, k], (d, flip(m, s & -s)))
+
+    def tile_next(k):
+        for bit in mp_bits[1:]:
+            for s in range(bit, nmp, 2 * bit):
+                for b in mp_bits:
+                    if b < bit:
+                        tile_copy(k, s | b).wait_recv()
+                        raw[k, across(s), :] += inbox[(s | b) - 1, k]
+                tile_copy(k, s).start()
 
     def tile(k):
         keys = p_ref if k == 0 else pbuf.at[k - 1]
@@ -168,24 +184,28 @@
             raw[k, at, :] = lax.dot_general(
                 q_ref[at, :], keys[...], (((1,), (1,)), ((), ())),
                 preferred_element_type=jnp.float32)
-        for j in range(1, nmp):
-            tile_copy(k, j).start()
+        for s in range(1, nmp, 2):
+            tile_copy(k, s).start()
 
     tile(0)
+    tile_next(0)
     ps.relay_two(odd)
     qs.start_own(even)
     ps.relay_one(odd)
     tile(2)
     tile(1)
+    tile_next(2)
+    tile_next(1)
     qs.relay_two(even)
     for c in range(CHUNKS):
         ps.arrived(2, c)
     tile(3)
+    tile_next(3)
     for k in range(1, WIN + 1):
         scale_copy(k).wait_recv()
     for k in (0, 2, 1, 3):
-        for j in range(1, nmp):
-            tile_copy(k, j).wait_recv()
+        for b in mp_bits:
+            tile_copy(k, b).wait_recv()
 
     lsum[...] = jnp.zeros_like(lsum)
 
@@ -195,18 +215,18 @@
         here = pl.ds(low, GROUP)
         whole = pl.ds(pl.multiple_of(m * share + low, GROUP), GROUP)
         row_scale = qs_ref[whole, :]
-        valid = ok_ref[whole, :] > 0.0
         cols = lax.broadcasted_iota(jnp.int32, (GROUP, rows), 1)
         ids = lax.broadcasted_iota(jnp.int32, (GROUP, rows), 0) + (m * share + low)
         diagonal = cols == ids
+        valid = ids[:, 0:1] < meta_ref[0]
         key_scale = [ps_ref[0:1, :]] + [psbuf[k, 0:1, :] for k in range(WIN)]
         scores = []
         for k in range(WIN + 1):
             s = raw[k, whole, :]
-            for j in range(nmp - 1):
-                s = s + inbox[j, k, here, :]
+            for b in mp_bits:
+                s = s + inbox[b - 1, k, here, :]
             scores.append(s * (row_scale * inv) * key_scale[k])
-        masked = [scores[k] + bias_ref[k:k + 1, :] for k in range(WIN + 1)]
+        masked = [jnp.where(cols < meta_ref[k], scores[k], -jnp.inf) for k in range(WIN + 1)]
         top = functools.reduce(jnp.maximum, [jnp.max(x, axis=1, keepdims=True) for x in masked])
         exps = [jnp.exp(x - top) for x in masked]
         total = sum(jnp.sum(x, axis=1, keepdims=True) for x in exps)
@@ -281,14 +301,29 @@
 
     local = Gather(weights, k_ss, k_rs)
     foreign = Gather(rw_in, g_ss, g_rs)
+    stages = [(d, flip(m, b)) for b in mp_bits] + [(flip(d, b), m) for b in dp_bits]
+
+    def loss_copy(i):
+        return copy(lsum.at[i], lin.at[i], l_ss.at[i], l_rs.at[i], stages[i])
+
+    def loss_step(i):
+        if i:
+            loss_copy(i - 1).wait_recv()
+            lsum[i] = lsum[i - 1] + lin[i - 1]
+        if i < len(stages):
+            loss_copy(i).start()
+
     local.begin()
+    loss_step(0)
     qs.relay_one(even)
+    loss_step(1)
     for k in range(1, WIN + 1):
         dispatch(k).wait_recv()
     foreign.begin()
+    loss_step(2)
     local.rest()
+    loss_step(3)
     local.all()
-    foreign.rest()
 
     @pl.loop(0, nmp)
     def _(r):
@@ -298,23 +333,17 @@
             out = out + jnp.dot(weights[k + 1, at, :], pbuf[k], preferred_element_type=jnp.float32)
         gq_ref[at, :] = out.astype(jnp.bfloat16)
 
+    loss_step(4)
+    foreign.rest()
     def back(w, x):
         return lax.dot_general(w, x, (((0,), (0,)), ((), ())), preferred_element_type=jnp.float32)
-
-    stages = [(d, flip(m, b)) for b in mp_bits] + [(flip(d, b), m) for b in dp_bits]
-
-    def loss_copy(i):
-        return copy(lsum.at[i], lin.at[i], l_ss.at[i], l_rs.at[i], stages[i])
-
-    for i in range(len(stages)):
-        loss_copy(i).start()
-        loss_copy(i).wait_recv()
-        lsum[i + 1] = lsum[i] + lin[i]
-    loss_ref[...] = lsum[len(stages)]
 
     for c in range(CHUNKS):
         qs.arrived(2, c)
     foreign.all()
+    for i in range(5, len(stages) + 1):
+        loss_step(i)
+    loss_ref[...] = lsum[len(stages), 0:1, 0:1] / meta_ref[WIN + 1].astype(jnp.float32)
     jc = 128
 
     @pl.loop(0, rows // jc)
@@ -349,9 +378,7 @@
     near = (mine + offsets) % ndp
     key_counts = jnp.sum(jnp.where(ids[None, :] == near[:, None], counts[None, :], 0), axis=1)
     live = (offsets == 0) | jnp.any(partners[0][None, :] == offsets[:, None], axis=1)
-    column = jnp.arange(rows, dtype=jnp.int32)
-    bias = jnp.where(live[:, None] & (column[None, :] < key_counts[:, None]), 0.0, -jnp.inf).astype(jnp.float32)
-    ok = (column < key_counts[0]).astype(jnp.float32)[:, None]
+    meta = jnp.concatenate([jnp.where(live, key_counts, 0), jnp.sum(counts)[None]]).astype(jnp.int32)
     ps = jnp.broadcast_to(passage_scale.astype(jnp.float32)[None, :], (8, rows))
     qs = query_scale.astype(jnp.float32)[:, None]
     nst = (ndp * nmp).bit_length() - 1
@@ -363,9 +390,9 @@
         out_shape=[
             jax.ShapeDtypeStruct((rows, width), bf),
             jax.ShapeDtypeStruct((rows, width), bf),
-            jax.ShapeDtypeStruct((8, 128), f32),
+            jax.ShapeDtypeStruct((1, 1), f32),
         ],
-        in_specs=[vm] * 6,
+        in_specs=[vm] * 4 + [pl.BlockSpec(memory_space=pltpu.SMEM)],
         out_specs=[vm] * 3,
         scratch_shapes=[
             pltpu.VMEM((WIN, rows, width), bf),
@@ -376,7 +403,6 @@
             pltpu.VMEM((WIN + 2, rows, rows), bf),
             pltpu.VMEM((WIN, share, rows), bf),
             pltpu.VMEM((WIN, rows, rows), bf),
-            pltpu.VMEM((8, 128), f32),
             pltpu.VMEM((nst + 1, 8, 128), f32),
             pltpu.VMEM((nst, 8, 128), f32),
             dma((4, CHUNKS)), dma((WIN, CHUNKS)),
@@ -390,8 +416,8 @@
         ],
         compiler_params=pltpu.CompilerParams(
             collective_id=0, has_side_effects=True, vmem_limit_bytes=56 * 1024 * 1024),
-    )(query, passage, ps, qs, ok, bias)
-    return loss[0, 0] / jnp.sum(counts).astype(f32), gq, gp
+    )(query, passage, ps, qs, meta)
+    return loss.reshape(()), gq, gp
 
 
 def solution(mesh):

time: 149 us -> 132 us (0.89)
  Pallas kernels: 135 us -> 120 us
    pallas_call x1, Pallas kernels: 135 us -> 120 us  [local(): pl.pallas_call(functools.partial(kernel, ndp, nmp, inv), out_shape=[jax.S...]
where the time goes in v2:
time: 132 us; the launch traced here: 131 us
  Pallas kernels  120 us (91%)
  local copies, waits for them, and re-layouts  6.78 us (5%)
  between operations  2.41 us (2%)
  other arithmetic  2.2 us (2%)
    pallas_call x1, Pallas kernels, local(): pl.pallas_call(functools.partial(kernel, ndp, nmp, inv), out_shape=[jax.S...  120 us
    unnamed x12, local copies, waits for them, and re-layouts  5.31 us

profile of v2, /device:TPU:0, one launch (start us, length us, event | category | flops | bytes accessed | tf_op | source)
XLA Modules:
  0.0 131.4 jit_solution(18408923796635732509)
XLA Ops:
  0.6 0.0 copy-start.3
  0.6 0.6 copy-done.3
  1.3 0.6 reduce_sum.19
  1.9 0.2 select_reduce_fusion
  2.1 0.0 copy-start.4
  2.1 0.7 copy-done.4
  2.8 0.1 fusion
  2.9 0.0 copy-start.1
  2.9 1.2 pad_add_fusion.meta_ref
  4.2 0.0 copy-done.1
  4.2 0.0 copy-start.2
  4.2 0.7 copy-done.2
  4.8 0.6 broadcast_in_dim.32.ps_ref
  5.5 0.9 copy.10.qs_ref
  6.3 120.0 %shard_map.85 = (bf16[512,1024]{1,0:T(8,128)(2,1)}, bf16[512,1024]{1,0:T(8,128)(2,1)}, f32[1,1]{1,0:T(1,128)}) custom-call(bf16[512,1024]{1,0:T(8,128)(2,1)} %q_ref.1, bf16[512,1024]{1,0:T(8,128)(2,1)} %p_ref.1, f32[8,512]{1,0:T(8,128)} %broadcast_in_dim.32.ps_ref, f32[512,1]{1,0:T(8,128)} %copy.10.qs_ref, s32[5]{0:T(128)} %pad_add_fusion.meta_ref), custom_call_target="tpu_custom_call" | custom-call | tf_op jit(solution)/shard_map/pallas_call | solution.py:388
  126.9 0.0 copy-start
  126.9 2.4 %copy.15 = bf16[512,1024]{1,0:T(8,128)(2,1)} copy(bf16[512,1024]{1,0:T(8,128)(2,1)} %get-tuple-element.13) | data formatting | bytes 2097152
  129.3 0.0 copy-done
  129.3 1.0 copy.16
  (3 shorter events, 0.0 us)
Async XLA Ops:
  0.6 0.7 copy-start.3
  2.1 0.7 copy-start.4
  2.9 1.3 copy-start.1
  4.2 0.7 copy-start.2
  126.9 2.4 %copy-start = (bf16[512,1024]{1,0:T(8,128)(2,1)S(1)}, bf16[512,1024]{1,0:T(8,128)(2,1)}, u32[]{:S(2)}) copy-start(bf16[512,1024]{1,0:T(8,128)(2,1)} %get-tuple-element.14) | copy-start | bytes 3145732

commit v3 on v2

--- a/solution.py
+++ b/solution.py
@@ -16,7 +16,7 @@
 
 def kernel(ndp, nmp, inv, q_ref, p_ref, ps_ref, qs_ref, meta_ref,
            gq_ref, gp_ref, loss_ref,
-           pbuf, qbuf, psbuf, raw, inbox, weights, rw_out, rw_in, lsum, lin,
+           pbuf, qbuf, psbuf, raw, inbox, weights, rw_out, rw_in, acc, lsum, lin,
            p_ss, p_rs, q_ss, q_rs, sc_ss, sc_rs, t_ss, t_rs, k_ss, k_rs,
            d_ss, d_rs, g_ss, g_rs, l_ss, l_rs):
     d = lax.axis_index("dp")
@@ -338,8 +338,6 @@
     def back(w, x):
         return lax.dot_general(w, x, (((0,), (0,)), ((), ())), preferred_element_type=jnp.float32)
 
-    for c in range(CHUNKS):
-        qs.arrived(2, c)
     foreign.all()
     for i in range(5, len(stages) + 1):
         loss_step(i)
@@ -350,8 +348,17 @@
     def _(t):
         at = pl.ds(pl.multiple_of(t * jc, jc), jc)
         out = back(weights[WIN + 1, :, at], q_ref[...])
-        for k in range(WIN):
+        for k in range(WIN - 1):
             out = out + back(rw_in[k, :, at], qbuf[k])
+        acc[at, :] = out
+
+    for c in range(CHUNKS):
+        qs.arrived(2, c)
+
+    @pl.loop(0, rows // jc)
+    def _(t):
+        at = pl.ds(pl.multiple_of(t * jc, jc), jc)
+        out = acc[at, :] + back(rw_in[WIN - 1, :, at], qbuf[WIN - 1])
         gp_ref[at, :] = out.astype(jnp.bfloat16)
 
     ps.finish(odd)
@@ -403,6 +410,7 @@
             pltpu.VMEM((WIN + 2, rows, rows), bf),
             pltpu.VMEM((WIN, share, rows), bf),
             pltpu.VMEM((WIN, rows, rows), bf),
+            pltpu.VMEM((rows, width), f32),
             pltpu.VMEM((nst + 1, 8, 128), f32),
             pltpu.VMEM((nst, 8, 128), f32),
             dma((4, CHUNKS)), dma((WIN, CHUNKS)),

time: 132 us -> 133 us (level)
  no operation moved by 1% of the time
where the time goes in v3:
time: 133 us; the launch traced here: 132 us
  Pallas kernels  121 us (91%)
  local copies, waits for them, and re-layouts  6.78 us (5%)
  between operations  2.41 us (2%)
  other arithmetic  2.2 us (2%)
    pallas_call x1, Pallas kernels, local(): pl.pallas_call(functools.partial(kernel, ndp, nmp, inv), out_shape=[jax.S...  121 us
    unnamed x12, local copies, waits for them, and re-layouts  5.31 us

profile of v3, /device:TPU:0, one launch (start us, length us, event | category | flops | bytes accessed | tf_op | source)
XLA Modules:
  0.0 132.2 jit_solution(12098347881019449692)
XLA Ops:
  0.6 0.0 copy-start.3
  0.6 0.6 copy-done.3
  1.3 0.6 reduce_sum.19
  1.9 0.2 select_reduce_fusion
  2.1 0.0 copy-start.4
  2.1 0.7 copy-done.4
  2.8 0.1 fusion
  2.9 0.0 copy-start.1
  2.9 1.2 pad_add_fusion.meta_ref
  4.2 0.0 copy-done.1
  4.2 0.0 copy-start.2
  4.2 0.7 copy-done.2
  4.8 0.6 broadcast_in_dim.32.ps_ref
  5.5 0.9 copy.10.qs_ref
  6.3 120.8 %shard_map.85 = (bf16[512,1024]{1,0:T(8,128)(2,1)}, bf16[512,1024]{1,0:T(8,128)(2,1)}, f32[1,1]{1,0:T(1,128)}) custom-call(bf16[512,1024]{1,0:T(8,128)(2,1)} %q_ref.1, bf16[512,1024]{1,0:T(8,128)(2,1)} %p_ref.1, f32[8,512]{1,0:T(8,128)} %broadcast_in_dim.32.ps_ref, f32[512,1]{1,0:T(8,128)} %copy.10.qs_ref, s32[5]{0:T(128)} %pad_add_fusion.meta_ref), custom_call_target="tpu_custom_call" | custom-call | tf_op jit(solution)/shard_map/pallas_call | solution.py:395
  127.7 0.0 copy-start
  127.8 2.4 %copy.15 = bf16[512,1024]{1,0:T(8,128)(2,1)} copy(bf16[512,1024]{1,0:T(8,128)(2,1)} %get-tuple-element.13) | data formatting | bytes 2097152
  130.1 0.0 copy-done
  130.1 1.0 copy.16
  (3 shorter events, 0.0 us)
Async XLA Ops:
  0.6 0.7 copy-start.3
  2.1 0.7 copy-start.4
  2.9 1.3 copy-start.1
  4.2 0.7 copy-start.2
  127.7 2.4 %copy-start = (bf16[512,1024]{1,0:T(8,128)(2,1)S(1)}, bf16[512,1024]{1,0:T(8,128)(2,1)}, u32[]{:S(2)}) copy-start(bf16[512,1024]{1,0:T(8,128)(2,1)} %get-tuple-element.14) | copy-start | bytes 3145732
